TPU v7x, 32 devices: a whole 2x2x4 slice. The times are simulated.
32 devices in a mesh: gz: 4 (over y, x), gy: 2 (over core), gx: 4 (over z).
Axes of the slice: x: 2, y: 2, z: 4, core: 2. Of those that a mesh axis runs over, the one named last changes fastest.
Arguments:
- populations: float32 [19, 32, 16, 512], P(None, 'gz', 'gy', 'gx'), may hold values from 0.1 to 20, as said below
- solid: int32 [32, 16, 512], P('gz', 'gy', 'gx'), may hold values 0 or 1
- ports: int32 [2, 16, 512], P(None, 'gy', 'gx'), may hold values 0 or 1
- concentration: float32 [2, 4, 2, 64], P(None, 'gz'), may hold values from 0 to 1
- loaded: float32 [2, 4, 2, 64], P(None, 'gz'), may hold values from 0 to 2
Outputs:
- final_populations: float32 [19, 32, 16, 512], P(None, 'gz', 'gy', 'gx')
- new_concentration: float32 [2, 4, 2, 64], P(None, 'gz')
- new_loaded: float32 [2, 4, 2, 64], P(None, 'gz')
Inputs may be any that keep to these rules, and one draw needn't show every extreme that they name: `populations`: every population is positive and of the size of its lattice weight times 36.
All inputs are finite; a program needn't handle non-finite values. No bound on the sum of `solid` or of `ports` on one device may be relied on, other than what follows from the above.
Results may differ from a plain program's by a relative error of at most 0.00002.
Values sent between devices are 32-bit elements; how exact they have to be, the bound alone decides.
A program may use at most 64 MiB of HBM per device.

v0:
```python
import jax
import jax.numpy as jnp
from jax import lax
from jax.sharding import PartitionSpec as P

ITERS = 2
lattice = [
    (0, 0, 0),
    (1, 0, 0),
    (-1, 0, 0),
    (0, 1, 0),
    (0, -1, 0),
    (0, 0, 1),
    (0, 0, -1),
    (1, 1, 0),
    (-1, -1, 0),
    (1, -1, 0),
    (-1, 1, 0),
    (1, 0, 1),
    (-1, 0, -1),
    (1, 0, -1),
    (-1, 0, 1),
    (0, 1, 1),
    (0, -1, -1),
    (0, 1, -1),
    (0, -1, 1),
]
opposite = [0, 2, 1, 4, 3, 6, 5, 8, 7, 10, 9, 12, 11, 14, 13, 16, 15, 18, 17]
weights = [1.0 / 3.0] + [1.0 / 18.0] * 6 + [1.0 / 36.0] * 12
relax_rate = 1.25
base_density = 36.0
inlet_speed = 0.05
spread_base = (0.03, 0.06)
spread_length = 0.1
uptake_rate = (0.3, 0.6)
affinity = (2.0, 0.5)
phase_ratio = 0.5
feed_level = (1.0, 0.5)


def extended(cells, sides, width, closed):
    for axis, dim in sides:
        count = lax.axis_size(axis)
        ends = count if closed else count - 1
        head = lax.slice_in_dim(cells, 0, width, axis=dim)
        tail = lax.slice_in_dim(cells, cells.shape[dim] - width, cells.shape[dim], axis=dim)
        cells = jnp.concatenate(
            [
                lax.ppermute(tail, axis, [(i, (i + 1) % count) for i in range(ends)]),
                cells,
                lax.ppermute(head, axis, [((i + 1) % count, i) for i in range(ends)]),
            ],
            axis=dim,
        )
    return cells


def equilibrium(density, velocity):
    speed_z, speed_y, speed_x = velocity
    square = speed_z * speed_z + speed_y * speed_y + speed_x * speed_x
    result = []
    for member in range(19):
        step_z, step_y, step_x = lattice[member]
        along = step_z * speed_z + step_y * speed_y + step_x * speed_x
        result.append(
            weights[member] * density * (1.0 + 3.0 * along + 4.5 * along * along - 1.5 * square)
        )
    return result


def moments(pops):
    density = pops[0]
    for member in range(1, 19):
        density = density + pops[member]
    flows = []
    for position in range(3):
        total = jnp.zeros_like(pops[0])
        for member in range(19):
            heading = lattice[member][position]
            if heading == 1:
                total = total + pops[member]
            elif heading == -1:
                total = total - pops[member]
        flows.append(total)
    return (density, flows)


def collide(pops, solid_flag):
    density, flows = moments(pops)
    velocity = [flow / density for flow in flows]
    balance = equilibrium(density, velocity)
    post = [
        jnp.where(
            solid_flag,
            pops[opposite[member]],
            pops[member] - relax_rate * (pops[member] - balance[member]),
        )
        for member in range(19)
    ]
    return (post, velocity)


def close_ends(moved, post, velocity, ports, first_dev, last_dev):
    inflow = equilibrium(base_density, (inlet_speed, 0.0, 0.0))
    outflow = equilibrium(base_density, (velocity[0][-1], velocity[1][-1], velocity[2][-1]))
    inlet_open = ports[0] == 1
    outlet_open = ports[1] == 1
    result = list(moved)
    for member in range(19):
        step_z = lattice[member][0]
        back = post[opposite[member]]
        if step_z == 1:
            entering = jnp.where(inlet_open, inflow[member], back[0])
            result[member] = (
                result[member].at[0].set(jnp.where(first_dev, entering, result[member][0]))
            )
        elif step_z == -1:
            entering = jnp.where(outlet_open, outflow[member], back[-1])
            result[member] = (
                result[member].at[-1].set(jnp.where(last_dev, entering, result[member][-1]))
            )
    return result


def block_sum(field):
    depth, height, width = field.shape
    return field.reshape(depth // 8, 8, height // 8, 8, width // 8, 8).sum(axis=(1, 3, 5))


def transport(padded, loaded, coarse_vel):
    centre = padded[:, 1:-1]
    neighbours = [
        (padded[:, :-2], padded[:, 2:]),
        (jnp.roll(centre, 1, axis=2), jnp.roll(centre, -1, axis=2)),
        (jnp.roll(centre, 1, axis=3), jnp.roll(centre, -1, axis=3)),
    ]
    change = jnp.zeros_like(centre)
    curvature = jnp.zeros_like(centre)
    reach = jnp.zeros_like(coarse_vel[0])
    for direction in range(3):
        courant = 8.0 * coarse_vel[direction]
        before, after = neighbours[direction]
        change = (
            change
            - jnp.maximum(courant, 0.0) * (centre - before)
            - jnp.minimum(courant, 0.0) * (after - centre)
        )
        curvature = curvature + after - 2.0 * centre + before
        reach = reach + jnp.abs(courant)
    base = jnp.array(spread_base, dtype=centre.dtype)[:, None, None, None]
    speed = jnp.array(uptake_rate, dtype=centre.dtype)[:, None, None, None]
    holding = jnp.array(affinity, dtype=centre.dtype)[:, None, None, None]
    rate = speed * (holding * centre - loaded)
    new_conc = centre + change + (base + spread_length * reach) * curvature - phase_ratio * rate
    return (new_conc, loaded + rate)


def body(populations, solid, ports, concentration, loaded):
    depth, height, width = solid.shape
    slab_pos = lax.axis_index("gz")
    first_dev = slab_pos == 0
    last_dev = slab_pos == lax.axis_size("gz") - 1
    pops = [populations[member] for member in range(19)]
    solid_flag = solid == 1
    for iteration in range(ITERS):
        post, velocity = collide(pops, solid_flag)
        padded = extended(jnp.stack(post), (("gz", 1), ("gy", 2), ("gx", 3)), 1, True)
        moved = []
        for member in range(19):
            step_z, step_y, step_x = lattice[member]
            moved.append(
                padded[
                    member,
                    1 - step_z : 1 - step_z + depth,
                    1 - step_y : 1 - step_y + height,
                    1 - step_x : 1 - step_x + width,
                ]
            )
        pops = close_ends(moved, post, velocity, ports, first_dev, last_dev)
    final = jnp.stack(pops)
    density, flows = moments(pops)
    fluid = (solid == 0).astype(jnp.float32)
    local = jnp.stack([block_sum(flow * fluid) for flow in flows]) / (512.0 * base_density)
    across = lax.all_gather(local, "gy", axis=2, tiled=True)
    coarse_vel = lax.all_gather(across, "gx", axis=3, tiled=True)
    padded_conc = extended(concentration, (("gz", 1),), 1, False)
    feed = jnp.broadcast_to(
        jnp.array(feed_level, dtype=jnp.float32)[:, None, None],
        (2, concentration.shape[2], concentration.shape[3]),
    )
    front = jnp.where(first_dev, feed, padded_conc[:, 0])
    rear = jnp.where(last_dev, concentration[:, -1], padded_conc[:, -1])
    padded_conc = padded_conc.at[:, 0].set(front).at[:, -1].set(rear)
    new_conc, new_load = transport(padded_conc, loaded, coarse_vel)
    return (final, new_conc, new_load)


def solution(mesh):
    placed = (
        P(None, "gz", "gy", "gx"),
        P("gz", "gy", "gx"),
        P(None, "gy", "gx"),
        P(None, "gz", None, None),
        P(None, "gz", None, None),
    )
    return jax.shard_map(
        body,
        mesh=mesh,
        in_specs=placed,
        out_specs=(P(None, "gz", "gy", "gx"), P(None, "gz", None, None), P(None, "gz", None, None)),
        check_vma=False,
    )
```

profile of v0, /device:TPU:0, one launch (start us, length us, event | category | flops | bytes accessed | tf_op | source)
XLA Modules:
  0.0 104.6 jit_solution(4216951791328130897)
XLA Ops:
  0.6 5.6 %collective-permute-start.12 = (f32[2,1,2,64]{3,2,1,0:T(2,128)}, f32[2,1,2,64]{3,2,1,0:T(2,128)}, u32[]{:S(2)}, u32[]{:S(2)}) collective-permute-start(f32[2,1,2,64]{3,2,1,0:T(2,128)} %param.56), channel_id=1, source_target_pairs={{0,8},{8,16},{16,24},{1,9},{9,17},{17,25},{2,10},{10,18},{18,26},{... | collective-permute-start | bytes 3080 | tf_op jit(solution)/shard_map/ppermute | solution.py:49
  6.2 1.3 %collective-permute-start.13 = (f32[2,1,2,64]{3,2,1,0:T(2,128)}, f32[2,1,2,64]{3,2,1,0:T(2,128)}, u32[]{:S(2)}, u32[]{:S(2)}) collective-permute-start(f32[2,1,2,64]{3,2,1,0:T(2,128)} %param.56), channel_id=1, source_target_pairs={{8,0},{16,8},{24,16},{9,1},{17,9},{25,17},{10,2},{18,10},{26,18},{... | collective-permute-start | bytes 3080 | tf_op jit(solution)/shard_map/ppermute | solution.py:51
  7.5 1.2 %constant_dynamic-update-slice_fusion.18 = (f32[19,8,8,128]{3,2,1,0:T(8,128)S(1)}, f32[8,8,128]{2,1,0:T(8,128)S(1)}, f32[8,8,128]{2,1,0:T(8,128)S(1)}, f32[8,8,1...) fusion(f32[19,8,8,128]{3,2,1,0:T(8,128)} %param.53, ...), kind=kLoop, calls=%fused_computation.20 | loop fusion | flops 589823 | bytes 860160
  9.5 0.8 constant_dynamic-update-slice_fusion.16
  11.8 2.7 %collective-permute-start = (f32[19,1,8,128]{3,2,1,0:T(8,128)S(1)}, f32[19,1,8,128]{3,2,1,0:T(8,128)S(1)}, u32[]{:S(2)}, u32[]{:S(2)}) collective-permute-start(f32[19,1,8,128]{3,2,1,0:T(8,128)S(1)} %get-tuple-element.383), channel_id=1, source_target_pairs={{0,8},{8,16},{16,24},{24,0},{1,9},{9,17},{17,25},{25,1},{2,10},{10... | collective-permute-start | bytes 233480 | tf_op jit(solution)/shard_map/ppermute | solution.py:49
  14.5 1.0 collective-permute-start.1
  16.2 2.4 %collective-permute-done = f32[19,1,8,128]{3,2,1,0:T(8,128)S(1)} collective-permute-done((f32[19,1,8,128]{3,2,1,0:T(8,128)S(1)}, f32[19,1,8,128]{3,2,1,0:T(8,128)S(1)}, u32[]{:S(2)}, u32[]{:S(2)}) %collective-permute-start) | collective-permute-done | bytes 77856 | tf_op jit(solution)/shard_map/ppermute | solution.py:49
  18.6 0.9 collective-permute-done.1
  21.5 1.7 %fusion.386 = (f32[19,10,10,1]{3,2,1,0:T(8,128)}, f32[19,10,10,1]{3,2,1,0:T(8,128)S(1)}) fusion(f32[19,10,10,128]{3,2,1,0:T(8,128)S(1)} %pad_maximum_fusion), kind=kLoop, calls=%fused_computation.679 | loop fusion | bytes 30400 | tf_op jit(solution)/shard_map/slice | solution.py:45
  23.2 2.1 %copy.55 = f32[19,10,10,1]{0,3,2,1:T(1,128)S(1)} copy(f32[19,10,10,1]{3,2,1,0:T(8,128)} %get-tuple-element.355) | data formatting | bytes 15200 | tf_op jit(solution)/shard_map/slice | solution.py:45
  25.4 3.6 %collective-permute-start.5 = (f32[19,10,10,1]{0,3,2,1:T(1,128)S(1)}, f32[19,10,10,1]{0,3,2,1:T(1,128)S(1)}, u32[]{:S(2)}, u32[]{:S(2)}) collective-permute-start(f32[19,10,10,1]{0,3,2,1:T(1,128)S(1)} %copy.55), channel_id=1, source_target_pairs={{1,0},{2,1},{3,2},{0,3},{5,4},{6,5},{7,6},{4,7},{9,8},{10,9},{11,1... | collective-permute-start | bytes 22808 | tf_op jit(solution)/shard_map/ppermute | solution.py:51
  29.9 1.1 %collective-permute-done.5 = f32[19,10,10,1]{0,3,2,1:T(1,128)S(1)} collective-permute-done((f32[19,10,10,1]{0,3,2,1:T(1,128)S(1)}, f32[19,10,10,1]{0,3,2,1:T(1,128)S(1)}, u32[]{:S(2)}, u32[]{:S(2)}) %collective-permute-start.5) | collective-permute-done | bytes 7632 | tf_op jit(solution)/shard_map/ppermute | solution.py:51
  31.0 1.6 %copy.56 = f32[19,10,10,1]{3,2,1,0:T(8,128)S(1)} copy(f32[19,10,10,1]{0,3,2,1:T(1,128)S(1)} %collective-permute-done.5) | data formatting | bytes 15200 | tf_op jit(solution)/shard_map/ppermute | solution.py:51
  32.7 3.0 %collective-permute-done.4 = f32[19,10,10,1]{0,3,2,1:T(1,128)S(1)} collective-permute-done((f32[19,10,10,1]{0,3,2,1:T(1,128)S(1)}, f32[19,10,10,1]{0,3,2,1:T(1,128)S(1)}, u32[]{:S(2)}, u32[]{:S(2)}) %collective-permute-start.4) | collective-permute-done | bytes 7632 | tf_op jit(solution)/shard_map/ppermute | solution.py:49
  35.7 2.7 %copy.54 = f32[19,10,10,1]{3,2,1,0:T(8,128)} copy(f32[19,10,10,1]{0,3,2,1:T(1,128)S(1)} %collective-permute-done.4) | data formatting | bytes 15200 | tf_op jit(solution)/shard_map/ppermute | solution.py:49
  38.4 1.0 maximum_bitcast_fusion.13
  39.5 1.3 %copy-done = f32[19,10,10,1]{3,2,1,0:T(8,128)S(1)} copy-done((f32[19,10,10,1]{3,2,1,0:T(8,128)S(1)}, f32[19,10,10,1]{3,2,1,0:T(8,128)}, u32[]{:S(2)}) %copy-start) | copy-done | bytes 7624
  48.5 2.1 %collective-permute-start.6 = (f32[19,1,8,128]{3,2,1,0:T(8,128)S(1)}, f32[19,1,8,128]{3,2,1,0:T(8,128)S(1)}, u32[]{:S(2)}, u32[]{:S(2)}) collective-permute-start(f32[19,1,8,128]{3,2,1,0:T(8,128)S(1)} %get-tuple-element.382), channel_id=1, source_target_pairs={{0,8},{8,16},{16,24},{24,0},{1,9},{9,17},{17,25},{25,1},{2,10},{10... | collective-permute-start | bytes 233480 | tf_op jit(solution)/shard_map/ppermute | solution.py:49
  50.6 0.8 collective-permute-start.7
  52.1 1.7 %collective-permute-done.6 = f32[19,1,8,128]{3,2,1,0:T(8,128)S(1)} collective-permute-done((f32[19,1,8,128]{3,2,1,0:T(8,128)S(1)}, f32[19,1,8,128]{3,2,1,0:T(8,128)S(1)}, u32[]{:S(2)}, u32[]{:S(2)}) %collective-permute-start.6) | collective-permute-done | bytes 77856 | tf_op jit(solution)/shard_map/ppermute | solution.py:49
  53.8 1.2 %collective-permute-done.7 = f32[19,1,8,128]{3,2,1,0:T(8,128)S(1)} collective-permute-done((f32[19,1,8,128]{3,2,1,0:T(8,128)S(1)}, f32[19,1,8,128]{3,2,1,0:T(8,128)S(1)}, u32[]{:S(2)}, u32[]{:S(2)}) %collective-permute-start.7) | collective-permute-done | bytes 77856 | tf_op jit(solution)/shard_map/ppermute | solution.py:51
  57.0 1.7 %fusion.385 = (f32[19,10,10,1]{3,2,1,0:T(8,128)S(1)}, f32[19,10,10,1]{3,2,1,0:T(8,128)}) fusion(f32[19,10,10,128]{3,2,1,0:T(8,128)S(1)} %pad_maximum_fusion.1), kind=kLoop, calls=%fused_computation.678 | loop fusion | bytes 30400 | tf_op jit(solution)/shard_map/slice | solution.py:45
  58.7 2.1 %copy.57 = f32[19,10,10,1]{0,3,2,1:T(1,128)S(1)} copy(f32[19,10,10,1]{3,2,1,0:T(8,128)} %get-tuple-element.354) | data formatting | bytes 15200 | tf_op jit(solution)/shard_map/slice | solution.py:46
  61.6 4.0 %collective-permute-start.11 = (f32[19,10,10,1]{0,3,2,1:T(1,128)S(1)}, f32[19,10,10,1]{0,3,2,1:T(1,128)}, u32[]{:S(2)}, u32[]{:S(2)}) collective-permute-start(f32[19,10,10,1]{0,3,2,1:T(1,128)S(1)} %copy.59), channel_id=1, source_target_pairs={{1,0},{2,1},{3,2},{0,3},{5,4},{6,5},{7,6},{4,7},{9,8},{10,9},{11,1... | collective-permute-start | bytes 22808 | tf_op jit(solution)/shard_map/ppermute | solution.py:51
  65.7 1.7 %collective-permute-done.11 = f32[19,10,10,1]{0,3,2,1:T(1,128)} collective-permute-done((f32[19,10,10,1]{0,3,2,1:T(1,128)S(1)}, f32[19,10,10,1]{0,3,2,1:T(1,128)}, u32[]{:S(2)}, u32[]{:S(2)}) %collective-permute-start.11) | collective-permute-done | bytes 7632 | tf_op jit(solution)/shard_map/ppermute | solution.py:51
  67.4 2.4 %copy.60 = f32[19,10,10,1]{3,2,1,0:T(8,128)S(1)} copy(f32[19,10,10,1]{0,3,2,1:T(1,128)} %collective-permute-done.11) | data formatting | bytes 15200 | tf_op jit(solution)/shard_map/ppermute | solution.py:51
  71.8 3.4 %copy.58 = f32[19,10,10,1]{3,2,1,0:T(8,128)} copy(f32[19,10,10,1]{0,3,2,1:T(1,128)} %collective-permute-done.10) | data formatting | bytes 15200 | tf_op jit(solution)/shard_map/ppermute | solution.py:49
  75.3 1.1 %maximum_bitcast_fusion.3 = (f32[8,8,128]{2,1,0:T(8,128)S(1)}, f32[8,8,128]{2,1,0:T(8,128)S(1)}, f32[8,8,128]{2,1,0:T(8,128)S(1)}) fusion(f32[19,10,10,1]{3,2,1,0:T(8,128)} %copy.58, f32[19,10,1,128]{3,2,1,0:T(1,128)S(1)} %collective-permute-done.9, f32[19,10,1,128]{3,2,1,0:T(1,128)S(1)} %collective-permute-done.8, ...), kind=kLoop, calls=%fused_computation.399 | loop fusion | flops 106496 | bytes 1078704 | tf_op jit(solution)/shard_map/squeeze | solution.py:172
  80.5 1.4 %select_reduce_fusion = (f32[128]{0:T(128)}, f32[128]{0:T(128)S(1)}, f32[128]{0:T(128)}, f32[1,8,8,128]{3,2,1,0:T(8,128)S(1)}, f32[1,8,8,128]{3,2,1,0:T(8,128)S(...) fusion(f32[8,8,128]{2,1,0:T(8,128)S(1)} %get-tuple-element.278,, ...), kind=kLoop, calls=%fused_computation.509 | loop fusion | flops 573056 | bytes 1612128 | tf_op jit(solution)/shard_map/reduce_sum | solution.py:127
  83.9 1.8 %all_gather.6 = f32[3,1,2,16]{3,1,0,2:T(1,128)S(1)} all-gather(f32[3,1,1,16]{3,1,0,2:T(1,128)S(1)} %fusion.358), channel_id=1, replica_groups=mesh['gz'=4,'gy'=2,'gx'=4] {'gy'}, dimensions={2}, use_global_device_ids=true | all-gather | bytes 576 | tf_op jit(solution)/shard_map/all_gather | solution.py:184
  85.8 13.6 %all_gather.7 = f32[3,1,2,64]{0,2,1,3:T(2,128)S(1)} all-gather(f32[3,1,2,16]{0,2,1,3:T(2,128)S(1)} %copy.62), channel_id=1, replica_groups=mesh['gz'=4,'gy'=2,'gx'=4] {'gx'}, dimensions={3}, use_global_device_ids=true | all-gather | bytes 1920 | tf_op jit(solution)/shard_map/all_gather | solution.py:185
  103.3 1.4 %multiply_subtract_fusion = f32[2,1,2,64]{3,2,1,0:T(2,128)} fusion(f32[2,1,2,64]{3,2,1,0:T(2,128)S(1)} %copy-done.9, f32[2,1,2,1]{3,2,1,0:T(2,128)S(1)} %copy-done.19, f32[2,1,2,63]{3,2,1,0:T(2,128)S(1)} %copy-done.21, f32[2,1,2,63]{3,2,1,0:T(2,128)S(1)} %copy-done.20, f32[2,1,2,1]{3,2,1,0:T(2,128)S(1)} %copy-done.18, f32[2,1,1,64]{3,2,1,0:T(1,128)S(1)} %copy-done.23, ...), kind=kLoop, calls=%fused_computation.666 | loop fusion | flops 10496 | bytes 11810 | tf_op jit(solution)/shard_map/sub | solution.py:154
  (170 shorter events, 28.7 us)
Async XLA Ops:
  0.6 10.5 %copy-start.2 = (f32[19,8,8,128]{3,2,1,0:T(8,128)S(1)}, f32[19,8,8,128]{3,2,1,0:T(8,128)}, u32[]{:S(2)}) copy-start(f32[19,8,8,128]{3,2,1,0:T(8,128)} %param.53) | copy-start | bytes 1867780
  0.6 102.5 %collective-permute-start.12 = (f32[2,1,2,64]{3,2,1,0:T(2,128)}, f32[2,1,2,64]{3,2,1,0:T(2,128)}, u32[]{:S(2)}, u32[]{:S(2)}) collective-permute-start(f32[2,1,2,64]{3,2,1,0:T(2,128)} %param.56), channel_id=1, source_target_pairs={{0,8},{8,16},{16,24},{1,9},{9,17},{17,25},{2,10},{10,18},{18,26},{... | collective-permute-start | bytes 3080 | tf_op jit(solution)/shard_map/ppermute | solution.py:49
  6.2 96.9 %collective-permute-start.13 = (f32[2,1,2,64]{3,2,1,0:T(2,128)}, f32[2,1,2,64]{3,2,1,0:T(2,128)}, u32[]{:S(2)}, u32[]{:S(2)}) collective-permute-start(f32[2,1,2,64]{3,2,1,0:T(2,128)} %param.56), channel_id=1, source_target_pairs={{8,0},{16,8},{24,16},{9,1},{17,9},{25,17},{10,2},{18,10},{26,18},{... | collective-permute-start | bytes 3080 | tf_op jit(solution)/shard_map/ppermute | solution.py:51
  11.3 4.3 %copy-start.8 = (f32[2,1,2,64]{3,2,1,0:T(2,128)S(1)}, f32[2,1,2,64]{3,2,1,0:T(2,128)}, u32[]{:S(2)}) copy-start(f32[2,1,2,64]{3,2,1,0:T(2,128)} %param.56) | copy-start | bytes 3076
  11.3 4.2 %copy-start.16 = (f32[2,1,2,64]{3,2,1,0:T(2,128)S(1)}, f32[2,1,2,64]{3,2,1,0:T(2,128)}, u32[]{:S(2)}) copy-start(f32[2,1,2,64]{3,2,1,0:T(2,128)} %param.57) | copy-start | bytes 3076
  11.8 6.8 %collective-permute-start = (f32[19,1,8,128]{3,2,1,0:T(8,128)S(1)}, f32[19,1,8,128]{3,2,1,0:T(8,128)S(1)}, u32[]{:S(2)}, u32[]{:S(2)}) collective-permute-start(f32[19,1,8,128]{3,2,1,0:T(8,128)S(1)} %get-tuple-element.383), channel_id=1, source_target_pairs={{0,8},{8,16},{16,24},{24,0},{1,9},{9,17},{17,25},{25,1},{2,10},{10... | collective-permute-start | bytes 233480 | tf_op jit(solution)/shard_map/ppermute | solution.py:49
  14.5 5.0 %collective-permute-start.1 = (f32[19,1,8,128]{3,2,1,0:T(8,128)S(1)}, f32[19,1,8,128]{3,2,1,0:T(8,128)S(1)}, u32[]{:S(2)}, u32[]{:S(2)}) collective-permute-start(f32[19,1,8,128]{3,2,1,0:T(8,128)S(1)} %get-tuple-element.384), channel_id=1, source_target_pairs={{8,0},{16,8},{24,16},{0,24},{9,1},{17,9},{25,17},{1,25},{10,2},{18... | collective-permute-start | bytes 233480 | tf_op jit(solution)/shard_map/ppermute | solution.py:51
  19.7 1.4 %collective-permute-start.2 = (f32[19,10,1,128]{3,2,1,0:T(1,128)S(1)}, f32[19,10,1,128]{3,2,1,0:T(1,128)S(1)}, u32[]{:S(2)}, u32[]{:S(2)}) collective-permute-start(f32[19,10,1,128]{3,2,1,0:T(1,128)S(1)} %get-tuple-element.375), channel_id=1, source_target_pairs={{0,4},{4,0},{1,5},{5,1},{2,6},{6,2},{3,7},{7,3},{8,12},{12,8},{9,1... | collective-permute-start | bytes 291848 | tf_op jit(solution)/shard_map/ppermute | solution.py:49
  19.8 1.4 %collective-permute-start.3 = (f32[19,10,1,128]{3,2,1,0:T(1,128)S(1)}, f32[19,10,1,128]{3,2,1,0:T(1,128)S(1)}, u32[]{:S(2)}, u32[]{:S(2)}) collective-permute-start(f32[19,10,1,128]{3,2,1,0:T(1,128)S(1)} %get-tuple-element.376), channel_id=1, source_target_pairs={{4,0},{0,4},{5,1},{1,5},{6,2},{2,6},{7,3},{3,7},{12,8},{8,12},{13,... | collective-permute-start | bytes 291848 | tf_op jit(solution)/shard_map/ppermute | solution.py:51
  25.4 4.5 %copy-start.15 = (s32[2,8,128]{2,1,0:T(8,128)S(1)}, s32[2,8,128]{2,1,0:T(8,128)}, u32[]{:S(2)}) copy-start(s32[2,8,128]{2,1,0:T(8,128)} %param.55) | copy-start | bytes 24580
  25.4 5.6 %collective-permute-start.5 = (f32[19,10,10,1]{0,3,2,1:T(1,128)S(1)}, f32[19,10,10,1]{0,3,2,1:T(1,128)S(1)}, u32[]{:S(2)}, u32[]{:S(2)}) collective-permute-start(f32[19,10,10,1]{0,3,2,1:T(1,128)S(1)} %copy.55), channel_id=1, source_target_pairs={{1,0},{2,1},{3,2},{0,3},{5,4},{6,5},{7,6},{4,7},{9,8},{10,9},{11,1... | collective-permute-start | bytes 22808 | tf_op jit(solution)/shard_map/ppermute | solution.py:51
  29.8 5.9 %collective-permute-start.4 = (f32[19,10,10,1]{0,3,2,1:T(1,128)S(1)}, f32[19,10,10,1]{0,3,2,1:T(1,128)S(1)}, u32[]{:S(2)}, u32[]{:S(2)}) collective-permute-start(f32[19,10,10,1]{0,3,2,1:T(1,128)S(1)} %copy.53), channel_id=1, source_target_pairs={{0,1},{1,2},{2,3},{3,0},{4,5},{5,6},{6,7},{7,4},{8,9},{9,10},{10,1... | collective-permute-start | bytes 22808 | tf_op jit(solution)/shard_map/ppermute | solution.py:49
  29.9 11.0 %copy-start.10 = (pred[1,8,128]{2,1,0:T(8,128)(4,1)}, pred[1,8,128]{2,1,0:T(8,128)(4,1)S(1)}, u32[]{:S(2)}) copy-start(pred[1,8,128]{2,1,0:T(8,128)(4,1)S(1)} %get-tuple-element.317) | copy-start | bytes 3076
  48.5 5.3 %collective-permute-start.6 = (f32[19,1,8,128]{3,2,1,0:T(8,128)S(1)}, f32[19,1,8,128]{3,2,1,0:T(8,128)S(1)}, u32[]{:S(2)}, u32[]{:S(2)}) collective-permute-start(f32[19,1,8,128]{3,2,1,0:T(8,128)S(1)} %get-tuple-element.382), channel_id=1, source_target_pairs={{0,8},{8,16},{16,24},{24,0},{1,9},{9,17},{17,25},{25,1},{2,10},{10... | collective-permute-start | bytes 233480 | tf_op jit(solution)/shard_map/ppermute | solution.py:49
  50.6 4.4 %collective-permute-start.7 = (f32[19,1,8,128]{3,2,1,0:T(8,128)S(1)}, f32[19,1,8,128]{3,2,1,0:T(8,128)S(1)}, u32[]{:S(2)}, u32[]{:S(2)}) collective-permute-start(f32[19,1,8,128]{3,2,1,0:T(8,128)S(1)} %get-tuple-element.381), channel_id=1, source_target_pairs={{8,0},{16,8},{24,16},{0,24},{9,1},{17,9},{25,17},{1,25},{10,2},{18... | collective-permute-start | bytes 233480 | tf_op jit(solution)/shard_map/ppermute | solution.py:51
  55.2 1.4 %collective-permute-start.8 = (f32[19,10,1,128]{3,2,1,0:T(1,128)S(1)}, f32[19,10,1,128]{3,2,1,0:T(1,128)S(1)}, u32[]{:S(2)}, u32[]{:S(2)}) collective-permute-start(f32[19,10,1,128]{3,2,1,0:T(1,128)S(1)} %get-tuple-element.371), channel_id=1, source_target_pairs={{0,4},{4,0},{1,5},{5,1},{2,6},{6,2},{3,7},{7,3},{8,12},{12,8},{9,1... | collective-permute-start | bytes 291848 | tf_op jit(solution)/shard_map/ppermute | solution.py:49
  55.2 1.4 %collective-permute-start.9 = (f32[19,10,1,128]{3,2,1,0:T(1,128)S(1)}, f32[19,10,1,128]{3,2,1,0:T(1,128)S(1)}, u32[]{:S(2)}, u32[]{:S(2)}) collective-permute-start(f32[19,10,1,128]{3,2,1,0:T(1,128)S(1)} %get-tuple-element.372), channel_id=1, source_target_pairs={{4,0},{0,4},{5,1},{1,5},{6,2},{2,6},{7,3},{3,7},{12,8},{8,12},{13,... | collective-permute-start | bytes 291848 | tf_op jit(solution)/shard_map/ppermute | solution.py:51
  60.8 10.4 %collective-permute-start.10 = (f32[19,10,10,1]{0,3,2,1:T(1,128)S(1)}, f32[19,10,10,1]{0,3,2,1:T(1,128)}, u32[]{:S(2)}, u32[]{:S(2)}) collective-permute-start(f32[19,10,10,1]{0,3,2,1:T(1,128)S(1)} %copy.57), channel_id=1, source_target_pairs={{0,1},{1,2},{2,3},{3,0},{4,5},{5,6},{6,7},{7,4},{8,9},{9,10},{10,1... | collective-permute-start | bytes 22808 | tf_op jit(solution)/shard_map/ppermute | solution.py:49
  61.6 5.8 %collective-permute-start.11 = (f32[19,10,10,1]{0,3,2,1:T(1,128)S(1)}, f32[19,10,10,1]{0,3,2,1:T(1,128)}, u32[]{:S(2)}, u32[]{:S(2)}) collective-permute-start(f32[19,10,10,1]{0,3,2,1:T(1,128)S(1)} %copy.59), channel_id=1, source_target_pairs={{1,0},{2,1},{3,2},{0,3},{5,4},{6,5},{7,6},{4,7},{9,8},{10,9},{11,1... | collective-permute-start | bytes 22808 | tf_op jit(solution)/shard_map/ppermute | solution.py:51
  81.8 21.2 %copy-start.6 = (f32[1,8,8,128]{3,2,1,0:T(8,128)S(1)}, f32[1,8,8,128]{3,2,1,0:T(8,128)}, u32[]{:S(2)}) copy-start(f32[1,8,8,128]{3,2,1,0:T(8,128)} %get-tuple-element.273) | copy-start | bytes 98308
  81.8 21.3 %copy-start.9 = (f32[2,1,2,64]{3,2,1,0:T(2,128)S(1)}, f32[2,1,2,64]{3,2,1,0:T(2,128)}, u32[]{:S(2)}) copy-start(f32[2,1,2,64]{3,2,1,0:T(2,128)} %param.56) | copy-start | bytes 3076
  81.8 21.3 %copy-start.17 = (f32[2,1,2,64]{3,2,1,0:T(2,128)S(1)}, f32[2,1,2,64]{3,2,1,0:T(2,128)}, u32[]{:S(2)}) copy-start(f32[2,1,2,64]{3,2,1,0:T(2,128)} %param.57) | copy-start | bytes 3076
  81.8 21.3 %copy-start.18 = (f32[2,1,2,1]{3,2,1,0:T(2,128)S(1)}, f32[2,1,2,1]{3,2,1,0:T(2,128)}, u32[]{:S(2)}) copy-start(f32[2,1,2,1]{3,2,1,0:T(2,128)} %get-tuple-element.394) | copy-start | bytes 52
  81.8 21.3 %copy-start.19 = (f32[2,1,2,1]{3,2,1,0:T(2,128)S(1)}, f32[2,1,2,1]{3,2,1,0:T(2,128)}, u32[]{:S(2)}) copy-start(f32[2,1,2,1]{3,2,1,0:T(2,128)} %get-tuple-element.395) | copy-start | bytes 52
  81.9 21.3 %copy-start.20 = (f32[2,1,2,63]{3,2,1,0:T(2,128)S(1)}, f32[2,1,2,63]{3,2,1,0:T(2,128)}, u32[]{:S(2)}) copy-start(f32[2,1,2,63]{3,2,1,0:T(2,128)} %get-tuple-element.396) | copy-start | bytes 3028
  81.9 21.3 %copy-start.21 = (f32[2,1,2,63]{3,2,1,0:T(2,128)S(1)}, f32[2,1,2,63]{3,2,1,0:T(2,128)}, u32[]{:S(2)}) copy-start(f32[2,1,2,63]{3,2,1,0:T(2,128)} %get-tuple-element.397) | copy-start | bytes 3028
  81.9 21.3 %copy-start.22 = (f32[2,1,1,64]{3,2,1,0:T(1,128)S(1)}, f32[2,1,1,64]{3,2,1,0:T(1,128)}, u32[]{:S(2)}) copy-start(f32[2,1,1,64]{3,2,1,0:T(1,128)} %get-tuple-element.392) | copy-start | bytes 1540
  81.9 21.3 %copy-start.23 = (f32[2,1,1,64]{3,2,1,0:T(1,128)S(1)}, f32[2,1,1,64]{3,2,1,0:T(1,128)}, u32[]{:S(2)}) copy-start(f32[2,1,1,64]{3,2,1,0:T(1,128)} %get-tuple-element.393) | copy-start | bytes 1540
  81.9 21.3 %copy-start.25 = (f32[2]{0:T(128)S(1)}, f32[2]{0:T(128)}, u32[]{:S(2)}) copy-start(f32[2]{0:T(128)} %constant.557.clone) | copy-start | bytes 28
  81.9 21.3 %copy-start.27 = (f32[2]{0:T(128)S(1)}, f32[2]{0:T(128)}, u32[]{:S(2)}) copy-start(f32[2]{0:T(128)} %constant.558.clone) | copy-start | bytes 28
  81.9 21.3 %copy-start.28 = (f32[2]{0:T(128)S(1)}, f32[2]{0:T(128)}, u32[]{:S(2)}) copy-start(f32[2]{0:T(128)} %constant.555.clone) | copy-start | bytes 28
  81.9 21.3 %copy-start.29 = (f32[2]{0:T(128)S(1)}, f32[2]{0:T(128)}, u32[]{:S(2)}) copy-start(f32[2]{0:T(128)} %constant.556.clone) | copy-start | bytes 28
  (12 other events, 20.7 us)
where the time goes:
time: 106 us; the launch traced here: 105 us
  local copies, waits for them, and re-layouts  29.9 us (28%)
  other arithmetic  22.8 us (22%)
  starting transfers between devices  22.4 us (21%)
  blocking collectives  15.5 us (15%)
  waiting for transfers between devices  12.7 us (12%)
  between operations  1.35 us (1%)
    all_gather x1, blocking collectives, body(): coarse_vel = lax.all_gather(across, 'gx', axis=3, tiled=True)  13.6 us
    ppermute x7, starting transfers between devices, extended(): lax.ppermute(head, axis, [((i + 1) % count, i) for i in range(ends)])  11.8 us
    unnamed x35, other arithmetic  10.8 us
    ppermute x7, starting transfers between devices, extended(): lax.ppermute(tail, axis, [(i, (i + 1) % count) for i in range(ends)])  10.6 us
    ppermute x7, waiting for transfers between devices, extended(): lax.ppermute(tail, axis, [(i, (i + 1) % count) for i in range(ends)])  7.47 us
    unnamed x82, local copies, waits for them, and re-layouts  6.83 us
    slice x5, local copies, waits for them, and re-layouts, extended(): head = lax.slice_in_dim(cells, 0, width, axis=dim)  6.35 us
    ppermute x2, local copies, waits for them, and re-layouts, extended(): lax.ppermute(tail, axis, [(i, (i + 1) % count) for i in range(ends)])  6.09 us
  transfers between devices with their start and end apart: 14, of which 11 were waited for; matrix products, arithmetic and copies ran while one was open for 46% of the time, Pallas kernels for 0%

commit v1 on v0

--- a/solution.py
+++ b/solution.py
@@ -38,6 +38,12 @@
 feed_level = (1.0, 0.5)
 
 
+def in_order(blocks, dim):
+    shape = list(blocks.shape[1:])
+    shape[dim] *= blocks.shape[0]
+    return jnp.moveaxis(blocks, 0, dim).reshape(shape)
+
+
 def extended(cells, sides, width, closed):
     for axis, dim in sides:
         count = lax.axis_size(axis)
@@ -182,7 +188,19 @@
     fluid = (solid == 0).astype(jnp.float32)
     local = jnp.stack([block_sum(flow * fluid) for flow in flows]) / (512.0 * base_density)
     across = lax.all_gather(local, "gy", axis=2, tiled=True)
-    coarse_vel = lax.all_gather(across, "gx", axis=3, tiled=True)
+    devices = lax.axis_size("gx")
+    pairs = [(i_2, (i_2 + 1) % devices) for i_2 in range(devices)]
+    back_2 = [(b, a) for a, b in pairs]
+    lower, upper = ([], [])
+    for step in range(devices - 1):
+        if step % 2 == 0:
+            lower.append(lax.ppermute(lower[-1] if lower else across, "gx", pairs))
+        else:
+            upper.append(lax.ppermute(upper[-1] if upper else across, "gx", back_2))
+    blocks = jnp.stack([*lower[::-1], across, *upper])
+    shift = lax.axis_index("gx") - len(lower)
+    blocks = blocks[(jnp.arange(devices) - shift) % devices]
+    coarse_vel = in_order(blocks, 3)
     padded_conc = extended(concentration, (("gz", 1),), 1, False)
     feed = jnp.broadcast_to(
         jnp.array(feed_level, dtype=jnp.float32)[:, None, None],

time: 106 us -> 102 us (0.962)
  blocking collectives: 15.5 us -> 1.83 us
  starting transfers between devices: 22.4 us -> 26.2 us
  waiting for transfers between devices: 12.7 us -> 15.8 us
  other arithmetic: 22.8 us -> 24.2 us
  local copies, waits for them, and re-layouts: 29.9 us -> 31.1 us
    all_gather x1 -> x0, blocking collectives: 13.6 us -> none  [body(): coarse_vel = lax.all_gather(across, 'gx', axis=3, tiled=True)]
    ppermute x0 -> x3, waiting for transfers between devices: none -> 5.32 us  [the longest x2 5.31 us: body(): lower.append(lax.ppermute(lower[-1] if lower else across, 'gx', pairs))]
    ppermute x0 -> x3, starting transfers between devices: none -> 3.92 us  [the longest x1 3.83 us: body(): upper.append(lax.ppermute(upper[-1] if upper else across, 'gx', back_2))]
    ppermute x2, local copies, waits for them, and re-layouts: 6.09 us -> 4.26 us  [extended(): lax.ppermute(tail, axis, [(i, (i + 1) % count) for i in range(ends)])]
    ppermute x7, waiting for transfers between devices: 5.23 us -> 3.44 us  [extended(): lax.ppermute(head, axis, [((i + 1) % count, i) for i in range(ends)])]
    unnamed x82 -> x53, local copies, waits for them, and re-layouts: 6.83 us -> 6.51 us
  transfers between devices with their start and end apart: 14 -> 17, of which waited for: 11 -> 12; matrix products, arithmetic and copies ran while one was open for 46% -> 52% of each run, Pallas kernels for 0% -> 0%
where the time goes in v1:
time: 102 us; the launch traced here: 100 us
  local copies, waits for them, and re-layouts  31.1 us (30%)
  starting transfers between devices  26.2 us (26%)
  other arithmetic  24.2 us (24%)
  waiting for transfers between devices  15.8 us (15%)
  blocking collectives  1.83 us (2%)
  between operations  1.2 us (1%)
    ppermute x7, starting transfers between devices, extended(): lax.ppermute(head, axis, [((i + 1) % count, i) for i in range(ends)])  11.6 us
    unnamed x35, other arithmetic  10.8 us
    ppermute x7, starting transfers between devices, extended(): lax.ppermute(tail, axis, [(i, (i + 1) % count) for i in range(ends)])  10.6 us
    ppermute x7, waiting for transfers between devices, extended(): lax.ppermute(tail, axis, [(i, (i + 1) % count) for i in range(ends)])  7.02 us
    slice x5, local copies, waits for them, and re-layouts, extended(): head = lax.slice_in_dim(cells, 0, width, axis=dim)  6.98 us
    unnamed x53, local copies, waits for them, and re-layouts  6.51 us
    ppermute x2, waiting for transfers between devices, body(): lower.append(lax.ppermute(lower[-1] if lower else across, 'gx', pairs))  5.31 us
    ppermute x2, local copies, waits for them, and re-layouts, extended(): lax.ppermute(head, axis, [((i + 1) % count, i) for i in range(ends)])  5.04 us
  transfers between devices with their start and end apart: 17, of which 12 were waited for; matrix products, arithmetic and copies ran while one was open for 52% of the time, Pallas kernels for 0%

profile of v1, /device:TPU:0, one launch (start us, length us, event | category | flops | bytes accessed | tf_op | source)
XLA Modules:
  0.0 100.3 jit_solution(13747544099414269072)
XLA Ops:
  0.6 5.6 %collective-permute-start.15 = (f32[2,1,2,64]{3,2,1,0:T(2,128)}, f32[2,1,2,64]{3,2,1,0:T(2,128)}, u32[]{:S(2)}, u32[]{:S(2)}) collective-permute-start(f32[2,1,2,64]{3,2,1,0:T(2,128)} %param.56), channel_id=1, source_target_pairs={{0,8},{8,16},{16,24},{1,9},{9,17},{17,25},{2,10},{10,18},{18,26},{... | collective-permute-start | bytes 3080 | tf_op jit(solution)/shard_map/ppermute | solution.py:55
  6.2 1.3 %collective-permute-start.16 = (f32[2,1,2,64]{3,2,1,0:T(2,128)}, f32[2,1,2,64]{3,2,1,0:T(2,128)}, u32[]{:S(2)}, u32[]{:S(2)}) collective-permute-start(f32[2,1,2,64]{3,2,1,0:T(2,128)} %param.56), channel_id=1, source_target_pairs={{8,0},{16,8},{24,16},{9,1},{17,9},{25,17},{10,2},{18,10},{26,18},{... | collective-permute-start | bytes 3080 | tf_op jit(solution)/shard_map/ppermute | solution.py:57
  7.5 1.2 %constant_dynamic-update-slice_fusion.18 = (f32[19,8,8,128]{3,2,1,0:T(8,128)S(1)}, f32[8,8,128]{2,1,0:T(8,128)S(1)}, f32[8,8,128]{2,1,0:T(8,128)S(1)}, f32[8,8,1...) fusion(f32[19,8,8,128]{3,2,1,0:T(8,128)} %param.53, ...), kind=kLoop, calls=%fused_computation.21 | loop fusion | flops 589823 | bytes 860160
  11.8 2.7 %collective-permute-start = (f32[19,1,8,128]{3,2,1,0:T(8,128)S(1)}, f32[19,1,8,128]{3,2,1,0:T(8,128)S(1)}, u32[]{:S(2)}, u32[]{:S(2)}) collective-permute-start(f32[19,1,8,128]{3,2,1,0:T(8,128)S(1)} %get-tuple-element.383), channel_id=1, source_target_pairs={{0,8},{8,16},{16,24},{24,0},{1,9},{9,17},{17,25},{25,1},{2,10},{10... | collective-permute-start | bytes 233480 | tf_op jit(solution)/shard_map/ppermute | solution.py:55
  14.5 1.0 %collective-permute-start.1 = (f32[19,1,8,128]{3,2,1,0:T(8,128)S(1)}, f32[19,1,8,128]{3,2,1,0:T(8,128)S(1)}, u32[]{:S(2)}, u32[]{:S(2)}) collective-permute-start(f32[19,1,8,128]{3,2,1,0:T(8,128)S(1)} %get-tuple-element.384), channel_id=1, source_target_pairs={{8,0},{16,8},{24,16},{0,24},{9,1},{17,9},{25,17},{1,25},{10,2},{18... | collective-permute-start | bytes 233480 | tf_op jit(solution)/shard_map/ppermute | solution.py:57
  17.5 1.1 %collective-permute-done = f32[19,1,8,128]{3,2,1,0:T(8,128)S(1)} collective-permute-done((f32[19,1,8,128]{3,2,1,0:T(8,128)S(1)}, f32[19,1,8,128]{3,2,1,0:T(8,128)S(1)}, u32[]{:S(2)}, u32[]{:S(2)}) %collective-permute-start) | collective-permute-done | bytes 77856 | tf_op jit(solution)/shard_map/ppermute | solution.py:55
  18.6 0.9 collective-permute-done.1
  21.5 1.7 %fusion.394 = (f32[19,10,10,1]{3,2,1,0:T(8,128)}, f32[19,10,10,1]{3,2,1,0:T(8,128)S(1)}) fusion(f32[19,10,10,128]{3,2,1,0:T(8,128)S(1)} %pad_maximum_fusion), kind=kLoop, calls=%fused_computation.696 | loop fusion | bytes 30400 | tf_op jit(solution)/shard_map/slice | solution.py:51
  23.2 2.1 %copy.88 = f32[19,10,10,1]{0,3,2,1:T(1,128)S(1)} copy(f32[19,10,10,1]{3,2,1,0:T(8,128)} %get-tuple-element.355) | data formatting | bytes 15200 | tf_op jit(solution)/shard_map/slice | solution.py:51
  25.4 3.6 %collective-permute-start.5 = (f32[19,10,10,1]{0,3,2,1:T(1,128)S(1)}, f32[19,10,10,1]{0,3,2,1:T(1,128)S(1)}, u32[]{:S(2)}, u32[]{:S(2)}) collective-permute-start(f32[19,10,10,1]{0,3,2,1:T(1,128)S(1)} %copy.88), channel_id=1, source_target_pairs={{1,0},{2,1},{3,2},{0,3},{5,4},{6,5},{7,6},{4,7},{9,8},{10,9},{11,1... | collective-permute-start | bytes 22808 | tf_op jit(solution)/shard_map/ppermute | solution.py:57
  29.9 1.0 %collective-permute-done.5 = f32[19,10,10,1]{0,3,2,1:T(1,128)S(1)} collective-permute-done((f32[19,10,10,1]{0,3,2,1:T(1,128)S(1)}, f32[19,10,10,1]{0,3,2,1:T(1,128)S(1)}, u32[]{:S(2)}, u32[]{:S(2)}) %collective-permute-start.5) | collective-permute-done | bytes 7632 | tf_op jit(solution)/shard_map/ppermute | solution.py:57
  31.0 1.6 %copy.89 = f32[19,10,10,1]{3,2,1,0:T(8,128)S(1)} copy(f32[19,10,10,1]{0,3,2,1:T(1,128)S(1)} %collective-permute-done.5) | data formatting | bytes 15200 | tf_op jit(solution)/shard_map/ppermute | solution.py:57
  32.7 3.0 %collective-permute-done.4 = f32[19,10,10,1]{0,3,2,1:T(1,128)S(1)} collective-permute-done((f32[19,10,10,1]{0,3,2,1:T(1,128)S(1)}, f32[19,10,10,1]{0,3,2,1:T(1,128)S(1)}, u32[]{:S(2)}, u32[]{:S(2)}) %collective-permute-start.4) | collective-permute-done | bytes 7632 | tf_op jit(solution)/shard_map/ppermute | solution.py:55
  35.7 2.7 %copy.87 = f32[19,10,10,1]{3,2,1,0:T(8,128)} copy(f32[19,10,10,1]{0,3,2,1:T(1,128)S(1)} %collective-permute-done.4) | data formatting | bytes 15200 | tf_op jit(solution)/shard_map/ppermute | solution.py:55
  38.4 1.0 maximum_bitcast_fusion.13
  39.5 1.3 %copy-done.1 = f32[19,10,10,1]{3,2,1,0:T(8,128)S(1)} copy-done((f32[19,10,10,1]{3,2,1,0:T(8,128)S(1)}, f32[19,10,10,1]{3,2,1,0:T(8,128)}, u32[]{:S(2)}) %copy-start.1) | copy-done | bytes 7624
  48.6 2.1 %collective-permute-start.6 = (f32[19,1,8,128]{3,2,1,0:T(8,128)S(1)}, f32[19,1,8,128]{3,2,1,0:T(8,128)S(1)}, u32[]{:S(2)}, u32[]{:S(2)}) collective-permute-start(f32[19,1,8,128]{3,2,1,0:T(8,128)S(1)} %get-tuple-element.382), channel_id=1, source_target_pairs={{0,8},{8,16},{16,24},{24,0},{1,9},{9,17},{17,25},{25,1},{2,10},{10... | collective-permute-start | bytes 233480 | tf_op jit(solution)/shard_map/ppermute | solution.py:55
  51.6 2.4 %collective-permute-done.6 = f32[19,1,8,128]{3,2,1,0:T(8,128)S(1)} collective-permute-done((f32[19,1,8,128]{3,2,1,0:T(8,128)S(1)}, f32[19,1,8,128]{3,2,1,0:T(8,128)S(1)}, u32[]{:S(2)}, u32[]{:S(2)}) %collective-permute-start.6) | collective-permute-done | bytes 77856 | tf_op jit(solution)/shard_map/ppermute | solution.py:55
  53.9 1.2 %collective-permute-done.7 = f32[19,1,8,128]{3,2,1,0:T(8,128)S(1)} collective-permute-done((f32[19,1,8,128]{3,2,1,0:T(8,128)S(1)}, f32[19,1,8,128]{3,2,1,0:T(8,128)S(1)}, u32[]{:S(2)}, u32[]{:S(2)}) %collective-permute-start.7) | collective-permute-done | bytes 77856 | tf_op jit(solution)/shard_map/ppermute | solution.py:57
  57.1 1.7 %fusion.393 = (f32[19,10,10,1]{3,2,1,0:T(8,128)S(1)}, f32[19,10,10,1]{3,2,1,0:T(8,128)}) fusion(f32[19,10,10,128]{3,2,1,0:T(8,128)S(1)} %pad_maximum_fusion.1), kind=kLoop, calls=%fused_computation.695 | loop fusion | bytes 30400 | tf_op jit(solution)/shard_map/slice | solution.py:51
  58.8 2.1 %copy.90 = f32[19,10,10,1]{0,3,2,1:T(1,128)S(1)} copy(f32[19,10,10,1]{3,2,1,0:T(8,128)} %get-tuple-element.354) | data formatting | bytes 15200 | tf_op jit(solution)/shard_map/slice | solution.py:52
  61.0 1.4 %copy.92 = f32[19,10,10,1]{0,3,2,1:T(1,128)} copy(f32[19,10,10,1]{3,2,1,0:T(8,128)S(1)} %get-tuple-element.353) | data formatting | bytes 15200 | tf_op jit(solution)/shard_map/slice | solution.py:51
  62.4 3.8 %collective-permute-start.11 = (f32[19,10,10,1]{0,3,2,1:T(1,128)}, f32[19,10,10,1]{0,3,2,1:T(1,128)}, u32[]{:S(2)}, u32[]{:S(2)}) collective-permute-start(f32[19,10,10,1]{0,3,2,1:T(1,128)} %copy.92), channel_id=1, source_target_pairs={{1,0},{2,1},{3,2},{0,3},{5,4},{6,5},{7,6},{4,7},{9,8},{10,9},{11,1... | collective-permute-start | bytes 22808 | tf_op jit(solution)/shard_map/ppermute | solution.py:57
  66.9 1.6 %copy.91 = f32[19,10,10,1]{3,2,1,0:T(8,128)S(1)} copy(f32[19,10,10,1]{0,3,2,1:T(1,128)S(1)} %collective-permute-done.10) | data formatting | bytes 15200 | tf_op jit(solution)/shard_map/ppermute | solution.py:55
  68.6 3.4 %copy.93 = f32[19,10,10,1]{3,2,1,0:T(8,128)} copy(f32[19,10,10,1]{0,3,2,1:T(1,128)} %collective-permute-done.11) | data formatting | bytes 15200 | tf_op jit(solution)/shard_map/ppermute | solution.py:57
  72.1 1.0 maximum_bitcast_fusion.2
  73.1 0.9 constant_dynamic-update-slice_fusion.57
  77.7 1.4 %select_reduce_fusion = (f32[128]{0:T(128)}, f32[128]{0:T(128)}, f32[128]{0:T(128)}, f32[1,8,8,128]{3,2,1,0:T(8,128)S(1)}, f32[1,8,8,128]{3,2,1,0:T(8,128)S(1)},...) fusion(f32[8,8,128]{2,1,0:T(8,128)S(1)} %get-tuple-element.278,, ...), kind=kLoop, calls=%fused_computation.510 | loop fusion | flops 573056 | bytes 1612128 | tf_op jit(solution)/shard_map/reduce_sum | solution.py:133
  81.6 1.8 %all_gather.3 = f32[3,1,2,16]{3,1,0,2:T(1,128)S(1)} all-gather(f32[3,1,1,16]{3,1,0,2:T(1,128)S(1)} %fusion.364), channel_id=1, replica_groups=mesh['gz'=4,'gy'=2,'gx'=4] {'gy'}, dimensions={2}, use_global_device_ids=true | all-gather | bytes 576 | tf_op jit(solution)/shard_map/all_gather | solution.py:190
  83.5 3.8 %collective-permute-start.14 = (f32[3,1,2,16]{3,1,0,2:T(1,128)S(1)}, f32[3,1,2,16]{3,1,0,2:T(1,128)S(1)}, u32[]{:S(2)}, u32[]{:S(2)}) collective-permute-start(f32[3,1,2,16]{3,1,0,2:T(1,128)S(1)} %all_gather.3), channel_id=1, source_target_pairs={{1,0},{2,1},{3,2},{0,3},{5,4},{6,5},{7,6},{4,7},{9,8},{10,9},{11,1... | collective-permute-start | bytes 1160 | tf_op jit(solution)/shard_map/ppermute | solution.py:199
  92.2 5.3 %collective-permute-done.13 = f32[3,1,2,16]{3,1,0,2:T(1,128)S(1)} collective-permute-done((f32[3,1,2,16]{3,1,0,2:T(1,128)S(1)}, f32[3,1,2,16]{3,1,0,2:T(1,128)S(1)}, u32[]{:S(2)}, u32[]{:S(2)}) %collective-permute-start.13) | collective-permute-done | bytes 416 | tf_op jit(solution)/shard_map/ppermute | solution.py:197
  98.8 1.4 %multiply_subtract_fusion = f32[2,1,2,64]{3,2,1,0:T(2,128)} fusion(f32[2,1,2,64]{3,2,1,0:T(2,128)S(1)} %copy-done.8, f32[2,1,2,1]{3,2,1,0:T(2,128)} %get-tuple-element.399, f32[2,1,2,63]{3,2,1,0:T(2,128)} %get-tuple-element.401, f32[2,1,2,63]{3,2,1,0:T(2,128)} %get-tuple-element.400, f32[2,1,2,1]{3,2,1,0:T(2,128)} %get-tuple-element.398, ...), kind=kLoop, calls=%fused_computation.687 | loop fusion | flops 10496 | bytes 11810 | tf_op jit(solution)/shard_map/sub | solution.py:160
  (160 shorter events, 31.7 us)
Async XLA Ops:
  0.6 10.5 %copy-start.2 = (f32[19,8,8,128]{3,2,1,0:T(8,128)S(1)}, f32[19,8,8,128]{3,2,1,0:T(8,128)}, u32[]{:S(2)}) copy-start(f32[19,8,8,128]{3,2,1,0:T(8,128)} %param.53) | copy-start | bytes 1867780
  0.6 98.1 %collective-permute-start.15 = (f32[2,1,2,64]{3,2,1,0:T(2,128)}, f32[2,1,2,64]{3,2,1,0:T(2,128)}, u32[]{:S(2)}, u32[]{:S(2)}) collective-permute-start(f32[2,1,2,64]{3,2,1,0:T(2,128)} %param.56), channel_id=1, source_target_pairs={{0,8},{8,16},{16,24},{1,9},{9,17},{17,25},{2,10},{10,18},{18,26},{... | collective-permute-start | bytes 3080 | tf_op jit(solution)/shard_map/ppermute | solution.py:55
  6.2 92.6 %collective-permute-start.16 = (f32[2,1,2,64]{3,2,1,0:T(2,128)}, f32[2,1,2,64]{3,2,1,0:T(2,128)}, u32[]{:S(2)}, u32[]{:S(2)}) collective-permute-start(f32[2,1,2,64]{3,2,1,0:T(2,128)} %param.56), channel_id=1, source_target_pairs={{8,0},{16,8},{24,16},{9,1},{17,9},{25,17},{10,2},{18,10},{26,18},{... | collective-permute-start | bytes 3080 | tf_op jit(solution)/shard_map/ppermute | solution.py:57
  11.3 4.3 %copy-start.7 = (f32[2,1,2,64]{3,2,1,0:T(2,128)S(1)}, f32[2,1,2,64]{3,2,1,0:T(2,128)}, u32[]{:S(2)}) copy-start(f32[2,1,2,64]{3,2,1,0:T(2,128)} %param.56) | copy-start | bytes 3076
  11.3 4.9 %copy-start.14 = (f32[2,1,2,64]{3,2,1,0:T(2,128)S(1)}, f32[2,1,2,64]{3,2,1,0:T(2,128)}, u32[]{:S(2)}) copy-start(f32[2,1,2,64]{3,2,1,0:T(2,128)} %param.57) | copy-start | bytes 3076
  11.3 4.9 %copy-start.15 = (f32[2]{0:T(128)S(1)}, f32[2]{0:T(128)}, u32[]{:S(2)}) copy-start(f32[2]{0:T(128)} %constant.577.clone) | copy-start | bytes 28
  11.3 4.9 %copy-start.16 = (f32[2]{0:T(128)S(1)}, f32[2]{0:T(128)}, u32[]{:S(2)}) copy-start(f32[2]{0:T(128)} %constant.578.clone) | copy-start | bytes 28
  11.8 6.8 %collective-permute-start = (f32[19,1,8,128]{3,2,1,0:T(8,128)S(1)}, f32[19,1,8,128]{3,2,1,0:T(8,128)S(1)}, u32[]{:S(2)}, u32[]{:S(2)}) collective-permute-start(f32[19,1,8,128]{3,2,1,0:T(8,128)S(1)} %get-tuple-element.383), channel_id=1, source_target_pairs={{0,8},{8,16},{16,24},{24,0},{1,9},{9,17},{17,25},{25,1},{2,10},{10... | collective-permute-start | bytes 233480 | tf_op jit(solution)/shard_map/ppermute | solution.py:55
  14.5 5.0 %collective-permute-start.1 = (f32[19,1,8,128]{3,2,1,0:T(8,128)S(1)}, f32[19,1,8,128]{3,2,1,0:T(8,128)S(1)}, u32[]{:S(2)}, u32[]{:S(2)}) collective-permute-start(f32[19,1,8,128]{3,2,1,0:T(8,128)S(1)} %get-tuple-element.384), channel_id=1, source_target_pairs={{8,0},{16,8},{24,16},{0,24},{9,1},{17,9},{25,17},{1,25},{10,2},{18... | collective-permute-start | bytes 233480 | tf_op jit(solution)/shard_map/ppermute | solution.py:57
  19.7 1.4 %collective-permute-start.2 = (f32[19,10,1,128]{3,2,1,0:T(1,128)S(1)}, f32[19,10,1,128]{3,2,1,0:T(1,128)S(1)}, u32[]{:S(2)}, u32[]{:S(2)}) collective-permute-start(f32[19,10,1,128]{3,2,1,0:T(1,128)S(1)} %get-tuple-element.375), channel_id=1, source_target_pairs={{0,4},{4,0},{1,5},{5,1},{2,6},{6,2},{3,7},{7,3},{8,12},{12,8},{9,1... | collective-permute-start | bytes 291848 | tf_op jit(solution)/shard_map/ppermute | solution.py:55
  19.8 1.4 %collective-permute-start.3 = (f32[19,10,1,128]{3,2,1,0:T(1,128)S(1)}, f32[19,10,1,128]{3,2,1,0:T(1,128)S(1)}, u32[]{:S(2)}, u32[]{:S(2)}) collective-permute-start(f32[19,10,1,128]{3,2,1,0:T(1,128)S(1)} %get-tuple-element.376), channel_id=1, source_target_pairs={{4,0},{0,4},{5,1},{1,5},{6,2},{2,6},{7,3},{3,7},{12,8},{8,12},{13,... | collective-permute-start | bytes 291848 | tf_op jit(solution)/shard_map/ppermute | solution.py:57
  25.4 4.5 %copy-start.13 = (s32[2,8,128]{2,1,0:T(8,128)S(1)}, s32[2,8,128]{2,1,0:T(8,128)}, u32[]{:S(2)}) copy-start(s32[2,8,128]{2,1,0:T(8,128)} %param.55) | copy-start | bytes 24580
  25.4 5.6 %collective-permute-start.5 = (f32[19,10,10,1]{0,3,2,1:T(1,128)S(1)}, f32[19,10,10,1]{0,3,2,1:T(1,128)S(1)}, u32[]{:S(2)}, u32[]{:S(2)}) collective-permute-start(f32[19,10,10,1]{0,3,2,1:T(1,128)S(1)} %copy.88), channel_id=1, source_target_pairs={{1,0},{2,1},{3,2},{0,3},{5,4},{6,5},{7,6},{4,7},{9,8},{10,9},{11,1... | collective-permute-start | bytes 22808 | tf_op jit(solution)/shard_map/ppermute | solution.py:57
  29.8 5.9 %collective-permute-start.4 = (f32[19,10,10,1]{0,3,2,1:T(1,128)S(1)}, f32[19,10,10,1]{0,3,2,1:T(1,128)S(1)}, u32[]{:S(2)}, u32[]{:S(2)}) collective-permute-start(f32[19,10,10,1]{0,3,2,1:T(1,128)S(1)} %copy.86), channel_id=1, source_target_pairs={{0,1},{1,2},{2,3},{3,0},{4,5},{5,6},{6,7},{7,4},{8,9},{9,10},{10,1... | collective-permute-start | bytes 22808 | tf_op jit(solution)/shard_map/ppermute | solution.py:55
  29.9 11.0 %copy-start.9 = (pred[1,8,128]{2,1,0:T(8,128)(4,1)}, pred[1,8,128]{2,1,0:T(8,128)(4,1)S(1)}, u32[]{:S(2)}) copy-start(pred[1,8,128]{2,1,0:T(8,128)(4,1)S(1)} %get-tuple-element.317) | copy-start | bytes 3076
  39.4 1.4 %copy-start.1 = (f32[19,10,10,1]{3,2,1,0:T(8,128)S(1)}, f32[19,10,10,1]{3,2,1,0:T(8,128)}, u32[]{:S(2)}) copy-start(f32[19,10,10,1]{3,2,1,0:T(8,128)} %copy.87) | copy-start | bytes 22804
  48.6 5.3 %collective-permute-start.6 = (f32[19,1,8,128]{3,2,1,0:T(8,128)S(1)}, f32[19,1,8,128]{3,2,1,0:T(8,128)S(1)}, u32[]{:S(2)}, u32[]{:S(2)}) collective-permute-start(f32[19,1,8,128]{3,2,1,0:T(8,128)S(1)} %get-tuple-element.382), channel_id=1, source_target_pairs={{0,8},{8,16},{16,24},{24,0},{1,9},{9,17},{17,25},{25,1},{2,10},{10... | collective-permute-start | bytes 233480 | tf_op jit(solution)/shard_map/ppermute | solution.py:55
  50.7 4.4 %collective-permute-start.7 = (f32[19,1,8,128]{3,2,1,0:T(8,128)S(1)}, f32[19,1,8,128]{3,2,1,0:T(8,128)S(1)}, u32[]{:S(2)}, u32[]{:S(2)}) collective-permute-start(f32[19,1,8,128]{3,2,1,0:T(8,128)S(1)} %get-tuple-element.381), channel_id=1, source_target_pairs={{8,0},{16,8},{24,16},{0,24},{9,1},{17,9},{25,17},{1,25},{10,2},{18... | collective-permute-start | bytes 233480 | tf_op jit(solution)/shard_map/ppermute | solution.py:57
  55.2 1.4 %collective-permute-start.8 = (f32[19,10,1,128]{3,2,1,0:T(1,128)S(1)}, f32[19,10,1,128]{3,2,1,0:T(1,128)S(1)}, u32[]{:S(2)}, u32[]{:S(2)}) collective-permute-start(f32[19,10,1,128]{3,2,1,0:T(1,128)S(1)} %get-tuple-element.371), channel_id=1, source_target_pairs={{0,4},{4,0},{1,5},{5,1},{2,6},{6,2},{3,7},{7,3},{8,12},{12,8},{9,1... | collective-permute-start | bytes 291848 | tf_op jit(solution)/shard_map/ppermute | solution.py:55
  55.3 1.4 %collective-permute-start.9 = (f32[19,10,1,128]{3,2,1,0:T(1,128)S(1)}, f32[19,10,1,128]{3,2,1,0:T(1,128)S(1)}, u32[]{:S(2)}, u32[]{:S(2)}) collective-permute-start(f32[19,10,1,128]{3,2,1,0:T(1,128)S(1)} %get-tuple-element.372), channel_id=1, source_target_pairs={{4,0},{0,4},{5,1},{1,5},{6,2},{2,6},{7,3},{3,7},{12,8},{8,12},{13,... | collective-permute-start | bytes 291848 | tf_op jit(solution)/shard_map/ppermute | solution.py:57
  60.9 6.0 %collective-permute-start.10 = (f32[19,10,10,1]{0,3,2,1:T(1,128)S(1)}, f32[19,10,10,1]{0,3,2,1:T(1,128)S(1)}, u32[]{:S(2)}, u32[]{:S(2)}) collective-permute-start(f32[19,10,10,1]{0,3,2,1:T(1,128)S(1)} %copy.90), channel_id=1, source_target_pairs={{0,1},{1,2},{2,3},{3,0},{4,5},{5,6},{6,7},{7,4},{8,9},{9,10},{10,1... | collective-permute-start | bytes 22808 | tf_op jit(solution)/shard_map/ppermute | solution.py:55
  62.4 6.3 %collective-permute-start.11 = (f32[19,10,10,1]{0,3,2,1:T(1,128)}, f32[19,10,10,1]{0,3,2,1:T(1,128)}, u32[]{:S(2)}, u32[]{:S(2)}) collective-permute-start(f32[19,10,10,1]{0,3,2,1:T(1,128)} %copy.92), channel_id=1, source_target_pairs={{1,0},{2,1},{3,2},{0,3},{5,4},{6,5},{7,6},{4,7},{9,8},{10,9},{11,1... | collective-permute-start | bytes 22808 | tf_op jit(solution)/shard_map/ppermute | solution.py:57
  72.1 1.0 %copy-start.10 = (pred[1,8,128]{2,1,0:T(8,128)(4,1)S(1)}, pred[1,8,128]{2,1,0:T(8,128)(4,1)}, u32[]{:S(2)}) copy-start(pred[1,8,128]{2,1,0:T(8,128)(4,1)} %copy-done.9) | copy-start | bytes 3076
  73.1 1.6 %copy-start = (f32[19,10,10,1]{3,2,1,0:T(8,128)S(1)}, f32[19,10,10,1]{3,2,1,0:T(8,128)}, u32[]{:S(2)}) copy-start(f32[19,10,10,1]{3,2,1,0:T(8,128)} %copy.93) | copy-start | bytes 22804
  74.0 1.5 %copy-start.12 = (pred[1,8,128]{2,1,0:T(8,128)(4,1)S(1)}, pred[1,8,128]{2,1,0:T(8,128)(4,1)}, u32[]{:S(2)}) copy-start(pred[1,8,128]{2,1,0:T(8,128)(4,1)} %copy-done.11) | copy-start | bytes 3076
  74.7 3.0 %copy-start.5 = (f32[8,8,128]{2,1,0:T(8,128)}, f32[8,8,128]{2,1,0:T(8,128)S(1)}, u32[]{:S(2)}) copy-start(f32[8,8,128]{2,1,0:T(8,128)S(1)} %constant_dynamic-update-slice_fusion.61) | copy-start | bytes 98308
  76.2 1.4 %copy-start.6 = (s32[8,8,128]{2,1,0:T(8,128)S(1)}, s32[8,8,128]{2,1,0:T(8,128)}, u32[]{:S(2)}) copy-start(s32[8,8,128]{2,1,0:T(8,128)} %param.54) | copy-start | bytes 98308
  77.7 21.1 %copy-start.8 = (f32[2,1,2,64]{3,2,1,0:T(2,128)S(1)}, f32[2,1,2,64]{3,2,1,0:T(2,128)}, u32[]{:S(2)}) copy-start(f32[2,1,2,64]{3,2,1,0:T(2,128)} %param.56) | copy-start | bytes 3076
  83.5 8.5 %collective-permute-start.12 = (f32[3,1,2,16]{3,1,0,2:T(1,128)S(1)}, f32[3,1,2,16]{3,1,0,2:T(1,128)S(1)}, u32[]{:S(2)}, u32[]{:S(2)}) collective-permute-start(f32[3,1,2,16]{3,1,0,2:T(1,128)S(1)} %all_gather.3), channel_id=1, source_target_pairs={{0,1},{1,2},{2,3},{3,0},{4,5},{5,6},{6,7},{7,4},{8,9},{9,10},{10,1... | collective-permute-start | bytes 1160 | tf_op jit(solution)/shard_map/ppermute | solution.py:197
  83.5 8.6 %collective-permute-start.14 = (f32[3,1,2,16]{3,1,0,2:T(1,128)S(1)}, f32[3,1,2,16]{3,1,0,2:T(1,128)S(1)}, u32[]{:S(2)}, u32[]{:S(2)}) collective-permute-start(f32[3,1,2,16]{3,1,0,2:T(1,128)S(1)} %all_gather.3), channel_id=1, source_target_pairs={{1,0},{2,1},{3,2},{0,3},{5,4},{6,5},{7,6},{4,7},{9,8},{10,9},{11,1... | collective-permute-start | bytes 1160 | tf_op jit(solution)/shard_map/ppermute | solution.py:199
  92.0 5.4 %collective-permute-start.13 = (f32[3,1,2,16]{3,1,0,2:T(1,128)S(1)}, f32[3,1,2,16]{3,1,0,2:T(1,128)S(1)}, u32[]{:S(2)}, u32[]{:S(2)}) collective-permute-start(f32[3,1,2,16]{3,1,0,2:T(1,128)S(1)} %collective-permute-done.12), channel_id=1, source_target_pairs={{0,1},{1,2},{2,3},{3,0},{4,5},{5,6},{6,7},{7,4},{8,9},{9,10},{10,1... | collective-permute-start | bytes 1160 | tf_op jit(solution)/shard_map/ppermute | solution.py:197
  92.1 8.2 %copy-start.3 = (f32[19,8,8,128]{3,2,1,0:T(8,128)}, f32[19,8,8,128]{3,2,1,0:T(8,128)S(1)}, u32[]{:S(2)}) copy-start(f32[19,8,8,128]{3,2,1,0:T(8,128)S(1)} %constant_dynamic-update-slice_fusion.38) | copy-start | bytes 1867780
  (2 other events, 1.5 us)
